TPU v7x, 128 devices: a whole 4x4x4 slice. The times are simulated.
128 devices in a mesh: neuron: 16 (over z, y), trial: 8 (over x, core).
Axes of the slice: x: 4, y: 4, z: 4, core: 2. Of those that a mesh axis runs over, the one named last changes fastest.
Arguments:
- drive: bfloat16 [8, 128, 131072], P(None, 'trial', 'neuron'), may hold values from -6 to 6
- learning: bfloat16 [8, 128, 131072], P(None, 'trial', 'neuron'), may hold values from -6 to 6
- membrane_init: float32 [128, 131072], P('trial', 'neuron'), may hold values from -3 to 3
- adapt_init: float32 [128, 131072], P('trial', 'neuron'), may hold values from 0 to 1
- trace_init: float32 [128, 131072], P('trial', 'neuron'), may hold values from 0 to 3
- membrane_decay: float32 [131072], P('neuron'), may hold values from 0.6 to 0.95
- adapt_decay: float32 [131072], P('neuron'), may hold values from 0.8 to 0.99
- adapt_gain: float32 [131072], P('neuron'), may hold values from 0.2 to 1
- threshold: float32 [131072], P('neuron'), may hold values from 0.5 to 1.5
- left_factor: bfloat16 [131072, 512], P('neuron'), may hold values from -6 to 6
- right_factor: bfloat16 [131072, 512], P('neuron'), may hold values from -16 to 16
Outputs:
- left_new: bfloat16 [131072, 512], P(('neuron', 'trial'))
- right_new: bfloat16 [131072, 512], P(('neuron', 'trial'))
All inputs are finite; a program needn't handle non-finite values.
Results may differ from a plain program's by a relative error of at most 0.0085.
Values may be sent and summed in bfloat16 or wider, within the bound.
No kernel may reach another device: no remote copies, remote signals or barrier semaphores. Data moves between devices by JAX's collectives and lax.ppermute only.
A program may use at most 128 MiB of HBM per device.

v0:
```python
import math

import jax
import jax.numpy as jnp
from jax import lax
from jax.sharding import PartitionSpec as P

sharpness = 3.0
learn_rate = 0.5


def rank_block(values, factor, weight):
    return jnp.dot(values, factor, preferred_element_type=jnp.float32) * weight


def shards(
    drive,
    learning,
    membrane_init,
    adapt_init,
    trace_init,
    membrane_decay,
    adapt_decay,
    adapt_gain,
    threshold,
    left_factor,
    right_factor,
):
    local_neurons = left_factor.shape[0]
    rank_width = left_factor.shape[1]
    step_count = drive.shape[0]
    neuron_count = local_neurons * lax.axis_size("neuron")
    norm_neurons = 1.0 / math.sqrt(neuron_count)
    norm_rank = 1.0 / math.sqrt(rank_width)
    membrane = membrane_init
    adaptation = adapt_init
    filtered = trace_init
    spikes = jax.nn.sigmoid(sharpness * (membrane - threshold - adapt_gain * adaptation))
    signals = []
    presyns = []
    g_blocks = []
    k_blocks = []
    for moment in range(step_count):
        partial_value = rank_block(spikes.astype(jnp.bfloat16), right_factor, norm_neurons)
        projected = lax.psum(partial_value, "neuron").astype(jnp.bfloat16)
        current = (
            lax.dot_general(
                projected, left_factor, (((1,), (1,)), ((), ())), preferred_element_type=jnp.float32
            )
            * norm_rank
        )
        membrane = (
            membrane_decay * membrane
            + drive[moment].astype(jnp.float32)
            + current
            - threshold * spikes
        )
        adaptation = adapt_decay * adaptation + spikes
        spikes = jax.nn.sigmoid(sharpness * (membrane - threshold - adapt_gain * adaptation))
        slope_value = sharpness * spikes * (1.0 - spikes)
        filtered = membrane_decay * filtered + spikes
        signal = (learning[moment].astype(jnp.float32) * slope_value).astype(jnp.bfloat16)
        presyn = filtered.astype(jnp.bfloat16)
        signals.append(signal)
        presyns.append(presyn)
        g_part = rank_block(presyn, right_factor, norm_neurons)
        k_part = rank_block(signal, left_factor, norm_neurons)
        g_total, k_total = lax.psum((g_part, k_part), "neuron")
        g_blocks.append(g_total.astype(jnp.bfloat16))
        k_blocks.append(k_total.astype(jnp.bfloat16))
    signal_all = jnp.stack(signals)
    presyn_all = jnp.stack(presyns)
    rank_g = jnp.stack(g_blocks)
    rank_k = jnp.stack(k_blocks)
    stored = local_neurons // lax.axis_size("trial")
    offset = lax.axis_index("trial") * stored
    left_rows = lax.dynamic_slice_in_dim(left_factor, offset, stored, 0).astype(jnp.float32)
    right_rows = lax.dynamic_slice_in_dim(right_factor, offset, stored, 0).astype(jnp.float32)
    contract_lead = (((0, 1), (0, 1)), ((), ()))
    signal_mine, presyn_mine = (
        lax.all_to_all(signal_all, "trial", split_axis=2, concat_axis=1, tiled=True),
        lax.all_to_all(presyn_all, "trial", split_axis=2, concat_axis=1, tiled=True),
    )
    first = lax.dot_general(
        signal_mine,
        lax.all_gather(rank_g, "trial", axis=1, tiled=True),
        contract_lead,
        preferred_element_type=jnp.float32,
    )
    second = lax.dot_general(
        presyn_mine,
        lax.all_gather(rank_k, "trial", axis=1, tiled=True),
        contract_lead,
        preferred_element_type=jnp.float32,
    )
    left_step = left_rows - learn_rate * (first * norm_rank)
    right_step = right_rows - learn_rate * (second * norm_rank)
    highest = lax.Precision.HIGHEST
    row_lead = (((0,), (0,)), ((), ()))
    gram_one = lax.psum(
        lax.dot_general(right_step, right_step, row_lead, precision=highest), ("neuron", "trial")
    )
    lower_one = jnp.linalg.cholesky(gram_one)
    basis = lax.linalg.triangular_solve(
        lower_one, right_step, left_side=False, lower=True, transpose_a=True
    )
    right_new = (basis * math.sqrt(neuron_count)).astype(jnp.bfloat16)
    left_new = (jnp.dot(left_step, lower_one, precision=highest) * norm_neurons).astype(
        jnp.bfloat16
    )
    return (left_new, right_new)


def solution(mesh):
    in_specs = (
        P(None, "trial", "neuron"),
        P(None, "trial", "neuron"),
        P("trial", "neuron"),
        P("trial", "neuron"),
        P("trial", "neuron"),
        P("neuron"),
        P("neuron"),
        P("neuron"),
        P("neuron"),
        P("neuron", None),
        P("neuron", None),
    )
    out_specs = (P(("neuron", "trial"), None), P(("neuron", "trial"), None))
    return jax.shard_map(shards, mesh=mesh, in_specs=in_specs, out_specs=out_specs, check_vma=False)
```

profile of v0, /device:TPU:1, one launch (start us, length us, event | category | flops | bytes accessed | tf_op | source)
XLA Modules:
  0.0 1214.8 jit_solution(1713676997602515515)
XLA Ops:
  12.3 62.5 %psum.175 = bf16[16,512]{1,0:T(8,128)(2,1)S(1)} all-reduce(f32[16,512]{1,0:T(8,128)S(1)} %convolution_multiply_fusion.31), channel_id=1, replica_groups=mesh['neuron'=16,'trial'=8] {'neuron'}, use_global_device_ids=true, to_apply=%region_0.0 | all-reduce | flops 8192 | bytes 49152 | tf_op jit(solution)/shard_map/psum | solution.py:45
  82.8 55.9 %psum.176 = bf16[16,512]{1,0:T(8,128)(2,1)S(1)} all-reduce(f32[16,512]{1,0:T(8,128)S(1)} %convolution_multiply_fusion.30), channel_id=1, replica_groups=mesh['neuron'=16,'trial'=8] {'neuron'}, use_global_device_ids=true, to_apply=%region_1.0 | all-reduce | flops 8192 | bytes 49152 | tf_op jit(solution)/shard_map/psum | solution.py:45
  150.7 56.0 %psum.177 = bf16[16,512]{1,0:T(8,128)(2,1)S(1)} all-reduce(f32[16,512]{1,0:T(8,128)S(1)} %convolution_multiply_fusion.29), channel_id=1, replica_groups=mesh['neuron'=16,'trial'=8] {'neuron'}, use_global_device_ids=true, to_apply=%region_2.0 | all-reduce | flops 8192 | bytes 49152 | tf_op jit(solution)/shard_map/psum | solution.py:45
  217.9 55.9 %psum.178 = bf16[16,512]{1,0:T(8,128)(2,1)S(1)} all-reduce(f32[16,512]{1,0:T(8,128)S(1)} %convolution_multiply_fusion.28), channel_id=1, replica_groups=mesh['neuron'=16,'trial'=8] {'neuron'}, use_global_device_ids=true, to_apply=%region_3.0 | all-reduce | flops 8192 | bytes 49152 | tf_op jit(solution)/shard_map/psum | solution.py:45
  287.2 56.4 %psum.179 = bf16[16,512]{1,0:T(8,128)(2,1)S(1)} all-reduce(f32[16,512]{1,0:T(8,128)S(1)} %convolution_multiply_fusion.27), channel_id=1, replica_groups=mesh['neuron'=16,'trial'=8] {'neuron'}, use_global_device_ids=true, to_apply=%region_4.0 | all-reduce | flops 8192 | bytes 49152 | tf_op jit(solution)/shard_map/psum | solution.py:45
  355.2 55.7 %psum.180 = bf16[16,512]{1,0:T(8,128)(2,1)S(1)} all-reduce(f32[16,512]{1,0:T(8,128)S(1)} %convolution_multiply_fusion.26), channel_id=1, replica_groups=mesh['neuron'=16,'trial'=8] {'neuron'}, use_global_device_ids=true, to_apply=%region_5.0 | all-reduce | flops 8192 | bytes 49152 | tf_op jit(solution)/shard_map/psum | solution.py:45
  425.3 56.5 %psum.181 = bf16[16,512]{1,0:T(8,128)(2,1)S(1)} all-reduce(f32[16,512]{1,0:T(8,128)} %convolution_multiply_fusion.25), channel_id=1, replica_groups=mesh['neuron'=16,'trial'=8] {'neuron'}, use_global_device_ids=true, to_apply=%region_6.0 | all-reduce | flops 8192 | bytes 49152 | tf_op jit(solution)/shard_map/psum | solution.py:45
  516.7 55.9 %psum.182 = bf16[16,512]{1,0:T(8,128)(2,1)S(1)} all-reduce(f32[16,512]{1,0:T(8,128)S(1)} %copy-done.39), channel_id=1, replica_groups=mesh['neuron'=16,'trial'=8] {'neuron'}, use_global_device_ids=true, to_apply=%region_7.0 | all-reduce | flops 8192 | bytes 49152 | tf_op jit(solution)/shard_map/psum | solution.py:45
  593.8 61.6 %all-reduce.6 = (bf16[16,512]{1,0:T(8,128)(2,1)S(1)}, bf16[16,512]{1,0:T(8,128)(2,1)S(1)}, bf16[16,512]{1,0:T(8,128)(2,1)S(1)}, bf16[16,512]{1,0:T(8,128)(2,1)S(...) all-reduce(f32[16,512]{1,0:T(8,128)S(1)} %convolution_multiply_fusi, ...), channel_id=1, replica_groups=mesh['neuron'=16,'trial'=8] {'neuron'}, use_global_device_ids=true, to_apply=%region_8.0 | all-reduce | flops 131072 | bytes 786432 | tf_op jit(solution)/shard_map/psum | solution.py:68
  656.1 13.1 %copy.34 = bf16[8,16,8192]{1,0,2:T(8,128)(2,1)} copy(bf16[8,16,8192]{2,1,0:T(8,128)(2,1)S(1)} %copy-done.19) | data formatting | bytes 4194304 | tf_op jit(solution)/shard_map/stack | solution.py:72
  669.3 19.6 %reshape.114 = bf16[8,2,65536]{2,1,0:T(2,128)(2,1)} reshape(bf16[8192,8,16]{2,1,0:T(8,128)(2,1)} %bitcast.266) | data formatting | bytes 4194304
  688.8 128.3 %all-to-all-start.1 = ((bf16[8,2,65536]{2,1,0:T(2,128)(2,1)}), bf16[8,2,65536]{2,1,0:T(2,128)(2,1)S(1)}, u32[]{:S(2)}, u32[]{:S(2)}) async-start(bf16[8,2,65536]{2,1,0:T(2,128)(2,1)} %reshape.114), calls=%async_computation.1 | async-start | bytes 4194304 | tf_op jit(solution)/shard_map/all_to_all | solution.py:82
  819.8 14.5 %copy.30 = bf16[8,16,8192]{1,0,2:T(8,128)(2,1)} copy(bf16[8,16,8192]{2,1,0:T(8,128)(2,1)} %bitcast_dynamic-update-slice_fusion.9) | data formatting | bytes 4194304 | tf_op jit(solution)/shard_map/stack | solution.py:71
  834.4 19.6 %reshape.112 = bf16[8,2,65536]{2,1,0:T(2,128)(2,1)} reshape(bf16[8192,8,16]{2,1,0:T(8,128)(2,1)} %bitcast.267) | data formatting | bytes 4194304
  858.7 13.1 %reshape.115 = bf16[8192,8,16]{2,1,0:T(8,128)(2,1)} reshape(bf16[8,2,65536]{2,1,0:T(2,128)(2,1)S(1)} %all-to-all-done.1) | data formatting | bytes 4194304
  871.8 17.1 %copy.36 = bf16[8,8,16,1024]{3,2,1,0:T(8,128)(2,1)} copy(bf16[8,8,16,1024]{2,0,3,1:T(8,128)(2,1)} %bitcast.268) | data formatting | bytes 4194304 | tf_op jit(solution)/shard_map/all_to_all | solution.py:82
  896.9 13.9 %reshape.113 = bf16[8192,8,16]{2,1,0:T(8,128)(2,1)} reshape(bf16[8,2,65536]{2,1,0:T(2,128)(2,1)} %all-to-all-done) | data formatting | bytes 4194304
  910.8 17.5 %copy.32 = bf16[8,8,16,1024]{3,2,1,0:T(8,128)(2,1)} copy(bf16[8,8,16,1024]{2,0,3,1:T(8,128)(2,1)} %bitcast.269) | data formatting | bytes 4194304 | tf_op jit(solution)/shard_map/all_to_all | solution.py:81
  932.8 109.1 %all-reduce.5.cloned.1.call-done = f32[512,512]{0,1:T(8,128)} async-done(((f32[512,512]{0,1:T(8,128)}), f32[512,512]{0,1:T(8,128)}) %all-reduce.5.cloned.1.call-update) | async-done | bytes 1048592 | tf_op jit(solution)/shard_map/psum | solution.py:100
  1047.0 11.7 cholesky.104
  1071.2 11.7 cholesky.217
  1118.1 11.9 cholesky.255
  1135.0 13.6 %while.1 = (s32[]{:T(128)}, f32[512,512]{1,0:T(8,128)}, s32[4,2]{0,1:T(2,128)S(1)}, f32[4,128,128]{2,1,0:T(8,128)}, s32[]{:T(128)}) while((s32[]{:T(128)}, f32[512,512]{1,0:T(8,128)}, s32[4,2]{0,1:T(2,128)S(1)}, f32[4,128,128]{2,1,0:T(8,128)}, s32[]{:T(128)}) %tuple.66), condition=%wide.while_cond, body=%wide.while_body.sunk | while | flops 2 | bytes 132705 | solution.py:104
  1148.7 40.1 %custom-call.33 = f32[4,128,128]{1,2,0:T(8,128)S(1)} custom-call(f32[4,128,128]{2,1,0:T(8,128)} %get-tuple-element.9), custom_call_target="InvertDiagBlocksLowerTriangular" | custom-call | tf_op jit(solution)/shard_map/triangular_solve | solution.py:104
  (209 shorter events, 239.9 us)
Async XLA Ops:
  7.2 67.7 %copy-start.11 = (f32[16,8192]{1,0:T(8,128)S(1)}, f32[16,8192]{1,0:T(8,128)}, u32[]{:S(2)}) copy-start(f32[16,8192]{1,0:T(8,128)} %param.13) | copy-start | bytes 1572868
  7.2 67.7 %copy-start.10 = (f32[16,8192]{1,0:T(8,128)S(1)}, f32[16,8192]{1,0:T(8,128)}, u32[]{:S(2)}) copy-start(f32[16,8192]{1,0:T(8,128)} %param.14) | copy-start | bytes 1572868
  7.2 67.7 %copy-start.17 = (f32[8192]{0:T(1024)S(1)}, f32[8192]{0:T(1024)}, u32[]{:S(2)}) copy-start(f32[8192]{0:T(1024)} %param.18) | copy-start | bytes 98308
  7.2 67.6 %copy-start.18 = (f32[8192]{0:T(1024)S(1)}, f32[8192]{0:T(1024)}, u32[]{:S(2)}) copy-start(f32[8192]{0:T(1024)} %param.19) | copy-start | bytes 98308
  7.2 67.6 %copy-start.25 = (f32[16,8192]{1,0:T(8,128)S(1)}, f32[16,8192]{1,0:T(8,128)}, u32[]{:S(2)}) copy-start(f32[16,8192]{1,0:T(8,128)} %param.15) | copy-start | bytes 1572868
  7.2 67.6 %copy-start.23 = (f32[8192]{0:T(1024)S(1)}, f32[8192]{0:T(1024)}, u32[]{:S(2)}) copy-start(f32[8192]{0:T(1024)} %param.16) | copy-start | bytes 98308
  7.2 67.6 %copy-start.24 = (f32[8192]{0:T(1024)S(1)}, f32[8192]{0:T(1024)}, u32[]{:S(2)}) copy-start(f32[8192]{0:T(1024)} %param.17) | copy-start | bytes 98308
  7.2 881.6 %all-gather.5.cloned.1.call-start = ((), (), s32[]{:S(2)}) async-start(), calls=%async_computation.3 | async-start | bytes 1179648 | tf_op jit(solution)/shard_map/all_gather | solution.py:92
  145.7 60.9 %copy-start.13 = (f32[16,8192]{1,0:T(8,128)}, f32[16,8192]{1,0:T(8,128)S(1)}, u32[]{:S(2)}) copy-start(f32[16,8192]{1,0:T(8,128)S(1)} %get-tuple-element.64) | copy-start | bytes 1572868
  145.7 128.1 %copy-start.2 = (f32[16,8192]{1,0:T(8,128)}, f32[16,8192]{1,0:T(8,128)S(1)}, u32[]{:S(2)}) copy-start(f32[16,8192]{1,0:T(8,128)S(1)} %get-tuple-element.62) | copy-start | bytes 1572868
  145.7 60.9 %copy-start.26 = (f32[16,8192]{1,0:T(8,128)S(1)}, f32[16,8192]{1,0:T(8,128)}, u32[]{:S(2)}) copy-start(f32[16,8192]{1,0:T(8,128)} %get-tuple-element.86) | copy-start | bytes 1572868
  213.3 60.5 %copy-start.14 = (f32[16,8192]{1,0:T(8,128)S(1)}, f32[16,8192]{1,0:T(8,128)}, u32[]{:S(2)}) copy-start(f32[16,8192]{1,0:T(8,128)} %copy-done.13) | copy-start | bytes 1572868
  282.6 61.0 %copy-start.4 = (f32[16,8192]{1,0:T(8,128)S(1)}, f32[16,8192]{1,0:T(8,128)}, u32[]{:S(2)}) copy-start(f32[16,8192]{1,0:T(8,128)} %get-tuple-element.55) | copy-start | bytes 1572868
  481.7 18.2 %slice-start.4 = ((s8[8388608]{0:T(1024)(128)(4,1)}), s8[4194304]{0:T(1024)(128)(4,1)S(1)}, s32[]{:S(2)}) async-start(s8[8388608]{0:T(1024)(128)(4,1)} %bitcast.264), calls=%async_computation.9 | async-start | bytes 8388608
  489.1 10.8 slice-start.5
  514.9 57.8 %copy-start.7 = (f32[16,8192]{1,0:T(8,128)S(1)}, f32[16,8192]{1,0:T(8,128)}, u32[]{:S(2)}) copy-start(f32[16,8192]{1,0:T(8,128)} %get-tuple-element.48) | copy-start | bytes 1572868
  514.9 57.8 %copy-start.9 = (f32[16,8192]{1,0:T(8,128)S(1)}, f32[16,8192]{1,0:T(8,128)}, u32[]{:S(2)}) copy-start(f32[16,8192]{1,0:T(8,128)} %copy-done.8) | copy-start | bytes 1572868
  514.9 57.8 %copy-start.12 = (f32[16,8192]{1,0:T(8,128)S(1)}, f32[16,8192]{1,0:T(8,128)}, u32[]{:S(2)}) copy-start(f32[16,8192]{1,0:T(8,128)} %get-tuple-element.50) | copy-start | bytes 1572868
  579.3 9.5 slice-start.2
  592.5 63.6 %copy-start.19 = (bf16[8,16,8192]{2,1,0:T(8,128)(2,1)S(1)}, bf16[8,16,8192]{2,1,0:T(8,128)(2,1)}, u32[]{:S(2)}) copy-start(bf16[8,16,8192]{2,1,0:T(8,128)(2,1)} %get-tuple-element.42) | copy-start | bytes 6291460
  688.8 165.1 %all-to-all-start.1 = ((bf16[8,2,65536]{2,1,0:T(2,128)(2,1)}), bf16[8,2,65536]{2,1,0:T(2,128)(2,1)S(1)}, u32[]{:S(2)}, u32[]{:S(2)}) async-start(bf16[8,2,65536]{2,1,0:T(2,128)(2,1)} %reshape.114), calls=%async_computation.1 | async-start | bytes 4194304 | tf_op jit(solution)/shard_map/all_to_all | solution.py:82
  817.1 111.2 %all-gather.3.cloned.1.call-start = ((), (), s32[]{:S(2)}) async-start(), calls=%async_computation.2 | async-start | bytes 1179648 | tf_op jit(solution)/shard_map/all_gather | solution.py:86
  853.9 42.9 %all-to-all-start = ((bf16[8,2,65536]{2,1,0:T(2,128)(2,1)}), bf16[8,2,65536]{2,1,0:T(2,128)(2,1)}, u32[]{:S(2)}, u32[]{:S(2)}) async-start(bf16[8,2,65536]{2,1,0:T(2,128)(2,1)} %reshape.112), calls=%async_computation | async-start | bytes 4194304 | tf_op jit(solution)/shard_map/all_to_all | solution.py:81
  858.7 183.2 %all-reduce.5.cloned.1.call-start = ((), (), s32[]{:S(2)}) async-start(), calls=%async_computation.4 | async-start | bytes 2097152 | tf_op jit(solution)/shard_map/psum | solution.py:100
  (27 other events, 64.5 us)
Sparse Core Ops, SparseCore 0:
  656.3 144.7 all-gather.4
  819.6 23.4 all-gather.2
  897.0 144.9 all-reduce.4
where the time goes:
time: 1230 us; the launch traced here: 1210 us
  blocking collectives  516 us (42%)
  matrix products  162 us (13%)
  local copies, waits for them, and re-layouts  149 us (12%)
  starting transfers between devices  133 us (11%)
  other arithmetic  127 us (10%)
  waiting for transfers between devices  109 us (9%)
  between operations  17.4 us (1%)
    psum x8, blocking collectives, shards(): projected = lax.psum(partial_value, 'neuron').astype(jnp.bfloat16)  455 us
    all_to_all x1, starting transfers between devices, shards(): lax.all_to_all(presyn_all, 'trial', split_axis=2, concat_axis=1, tiled=True)  128 us
    psum x1, waiting for transfers between devices, shards(): lax.psum(lax.dot_general(right_step, right_step, row_lead, precision=high...  109 us
    another operation x14, other arithmetic, shards(): lower_one = jnp.linalg.cholesky(gram_one)  78.7 us
    dot_general x24, matrix products, rank_block(): return jnp.dot(values, factor, preferred_element_type=jnp.float32) * weight  71.5 us
    unnamed x111, local copies, waits for them, and re-layouts  70.7 us
    psum x1, blocking collectives, shards(): g_total, k_total = lax.psum((g_part, k_part), 'neuron')  61.6 us
    dot_general x8, matrix products, shards(): lax.dot_general(projected, left_factor, (((1,), (1,)), ((), ())), preferr...  55.8 us
  transfers between devices with their start and end apart: 5, of which 1 were waited for; matrix products, arithmetic and copies ran while one was open for 12% of the time, Pallas kernels for 0%

commit v1 on v0

v1 whole, which is shorter than its diff:
```python
import math

import jax
import jax.numpy as jnp
from jax import lax
from jax.sharding import PartitionSpec as P

sharpness = 3.0
learn_rate = 0.5


def rank_block(values, factor, weight):
    return jnp.dot(values, factor, preferred_element_type=jnp.float32) * weight


def swap(values, axes):
    return lax.all_to_all(values, axes, split_axis=0, concat_axis=0, tiled=True)


def spread(values, axes):
    copies = math.prod(lax.axis_size(a) for a in ((axes,) if isinstance(axes, str) else axes))
    return swap(jnp.broadcast_to(values[None], (copies,) + values.shape), axes)


def total(partial_value, axes):
    return jnp.sum(spread(partial_value.astype(jnp.bfloat16), axes).astype(jnp.float32), 0)


def shards(
    drive,
    learning,
    membrane_init,
    adapt_init,
    trace_init,
    membrane_decay,
    adapt_decay,
    adapt_gain,
    threshold,
    left_factor,
    right_factor,
):
    local_neurons = left_factor.shape[0]
    rank_width = left_factor.shape[1]
    step_count, local_trials = drive.shape[:2]
    neuron_shards = lax.axis_size("neuron")
    trial_shards = lax.axis_size("trial")
    neuron_count = local_neurons * neuron_shards
    norm_neurons = 1.0 / math.sqrt(neuron_count)
    norm_rank = 1.0 / math.sqrt(rank_width)
    membrane = membrane_init
    adaptation = adapt_init
    filtered = trace_init
    spikes = jax.nn.sigmoid(sharpness * (membrane - threshold - adapt_gain * adaptation))
    signals = []
    presyns = []
    for moment in range(step_count):
        partial_value = rank_block(spikes.astype(jnp.bfloat16), right_factor, norm_neurons)
        projected = total(partial_value, "neuron").astype(jnp.bfloat16)
        current = (
            lax.dot_general(
                projected, left_factor, (((1,), (1,)), ((), ())), preferred_element_type=jnp.float32
            )
            * norm_rank
        )
        membrane = (
            membrane_decay * membrane
            + drive[moment].astype(jnp.float32)
            + current
            - threshold * spikes
        )
        adaptation = adapt_decay * adaptation + spikes
        spikes = jax.nn.sigmoid(sharpness * (membrane - threshold - adapt_gain * adaptation))
        slope_value = sharpness * spikes * (1.0 - spikes)
        filtered = membrane_decay * filtered + spikes
        signals.append((learning[moment].astype(jnp.float32) * slope_value).astype(jnp.bfloat16))
        presyns.append(filtered.astype(jnp.bfloat16))
    rows = step_count * local_trials
    stored = local_neurons // trial_shards
    signal_all = jnp.concatenate(signals)
    presyn_all = jnp.concatenate(presyns)
    g_part = rank_block(presyn_all, right_factor, norm_neurons)
    k_part = rank_block(signal_all, left_factor, norm_neurons)
    both = jnp.concatenate([g_part, k_part]).astype(jnp.bfloat16)
    mine = swap(both.reshape(neuron_shards, -1, rank_width), "neuron")
    mine = jnp.sum(mine.astype(jnp.float32), 0).astype(jnp.bfloat16)
    ranks = spread(mine, "neuron").reshape(2 * rows, rank_width)
    ranks = spread(ranks, "trial")
    rank_g = ranks[:, :rows].reshape(-1, rank_width)
    rank_k = ranks[:, rows:].reshape(-1, rank_width)

    def by_stored(values):
        pieces = values.reshape(rows, trial_shards, stored).transpose(1, 0, 2)
        return swap(pieces, "trial").reshape(-1, stored)

    signal_mine = by_stored(signal_all)
    presyn_mine = by_stored(presyn_all)
    offset = lax.axis_index("trial") * stored
    left_rows = lax.dynamic_slice_in_dim(left_factor, offset, stored, 0).astype(jnp.float32)
    right_rows = lax.dynamic_slice_in_dim(right_factor, offset, stored, 0).astype(jnp.float32)
    lead = (((0,), (0,)), ((), ()))
    first = lax.dot_general(signal_mine, rank_g, lead, preferred_element_type=jnp.float32)
    second = lax.dot_general(presyn_mine, rank_k, lead, preferred_element_type=jnp.float32)
    left_step = left_rows - learn_rate * (first * norm_rank)
    right_step = right_rows - learn_rate * (second * norm_rank)
    highest = lax.Precision.HIGHEST
    gram_part = lax.dot_general(right_step, right_step, lead, precision=highest)
    everyone = ("neuron", "trial")
    gram_mine = jnp.sum(
        swap(gram_part.reshape(neuron_shards * trial_shards, -1, rank_width), everyone), 0
    )
    gram_one = spread(gram_mine, everyone).reshape(rank_width, rank_width)
    lower_one = jnp.linalg.cholesky(gram_one)
    basis = lax.linalg.triangular_solve(
        lower_one, right_step, left_side=False, lower=True, transpose_a=True
    )
    right_new = (basis * math.sqrt(neuron_count)).astype(jnp.bfloat16)
    left_new = (jnp.dot(left_step, lower_one, precision=highest) * norm_neurons).astype(
        jnp.bfloat16
    )
    return (left_new, right_new)


def solution(mesh):
    in_specs = (
        P(None, "trial", "neuron"),
        P(None, "trial", "neuron"),
        P("trial", "neuron"),
        P("trial", "neuron"),
        P("trial", "neuron"),
        P("neuron"),
        P("neuron"),
        P("neuron"),
        P("neuron"),
        P("neuron", None),
        P("neuron", None),
    )
    out_specs = (P(("neuron", "trial"), None), P(("neuron", "trial"), None))
    return jax.shard_map(shards, mesh=mesh, in_specs=in_specs, out_specs=out_specs, check_vma=False)
```

time: 1230 us -> 563 us (0.46)
  blocking collectives: 516 us -> 123 us
  local copies, waits for them, and re-layouts: 149 us -> 31.9 us
  starting transfers between devices: 133 us -> 30.8 us
  matrix products: 162 us -> 136 us
  between operations: 17.4 us -> 3.88 us
    psum x9 -> x0, blocking collectives: 516 us -> none  [the longest x8 455 us: shards(): projected = lax.psum(partial_value, 'neuron').astype(jnp.bfloat16)]
    all_to_all x0 -> x8, blocking collectives: none -> 123 us  [swap(): return lax.all_to_all(values, axes, split_axis=0, concat_axis=0, tiled=True)]
    psum x1 -> x0, waiting for transfers between devices: 109 us -> none  [shards(): lax.psum(lax.dot_general(right_step, right_step, row_lead, precision=high...]
    all_to_all x2 -> x7, waiting for transfers between devices: 0.01 us -> 102 us  [swap(): return lax.all_to_all(values, axes, split_axis=0, concat_axis=0, tiled=True)]
    all_to_all x2 -> x7, starting transfers between devices: 133 us -> 30.8 us  [swap(): return lax.all_to_all(values, axes, split_axis=0, concat_axis=0, tiled=True)]
    unnamed x111 -> x39, local copies, waits for them, and re-layouts: 70.7 us -> 3.03 us
    all_to_all x2 -> x0, local copies, waits for them, and re-layouts: 34.6 us -> none  [the longest x1 17.5 us: shards(): lax.all_to_all(signal_all, 'trial', split_axis=2, concat_axis=1, tiled=True)]
    another operation x16 -> x12, local copies, waits for them, and re-layouts: 41.3 us -> 13.8 us  [the longest x1 14.5 us: shards(): signal_all = jnp.stack(signals)]
  transfers between devices with their start and end apart: 5 -> 7, of which waited for: 1 -> 7; matrix products, arithmetic and copies ran while one was open for 12% -> 2% of each run, Pallas kernels for 0% -> 0%
where the time goes in v1:
time: 563 us; the launch traced here: 553 us
  matrix products  136 us (24%)
  other arithmetic  126 us (22%)
  blocking collectives  123 us (22%)
  waiting for transfers between devices  102 us (18%)
  local copies, waits for them, and re-layouts  31.9 us (6%)
  starting transfers between devices  30.8 us (5%)
    all_to_all x8, blocking collectives, swap(): return lax.all_to_all(values, axes, split_axis=0, concat_axis=0, tiled=True)  123 us
    all_to_all x7, waiting for transfers between devices, swap(): return lax.all_to_all(values, axes, split_axis=0, concat_axis=0, tiled=True)  102 us
    another operation x14, other arithmetic, shards(): lower_one = jnp.linalg.cholesky(gram_one)  79 us
    dot_general x8, matrix products, shards(): lax.dot_general(projected, left_factor, (((1,), (1,)), ((), ())), preferr...  57.2 us
    dot_general x10, matrix products, rank_block(): return jnp.dot(values, factor, preferred_element_type=jnp.float32) * weight  44.6 us
    another operation x3, other arithmetic, shards(): lax.linalg.triangular_solve(lower_one, right_step, left_side=False, lower...  41.2 us
    all_to_all x7, starting transfers between devices, swap(): return lax.all_to_all(values, axes, split_axis=0, concat_axis=0, tiled=True)  30.8 us
    another operation x12, local copies, waits for them, and re-layouts  13.8 us
  transfers between devices with their start and end apart: 7, of which 7 were waited for; matrix products, arithmetic and copies ran while one was open for 2% of the time, Pallas kernels for 0%

profile of v1, /device:TPU:1, one launch (start us, length us, event | category | flops | bytes accessed | tf_op | source)
XLA Modules:
  0.0 553.0 jit_solution(6756839884583172756)
XLA Ops:
  5.8 15.9 %all_to_all.75 = bf16[16,16,512]{2,1,0:T(8,128)(2,1)S(1)} all-to-all(bf16[16,16,512]{2,1,0:T(8,128)(2,1)S(1)} %broadcast_in_dim.25), channel_id=1, replica_groups=mesh['neuron'=16,'trial'=8] {'neuron'}, dimensions={0} | all-to-all | bytes 524288 | tf_op jit(solution)/shard_map/all_to_all | solution.py:17
  33.2 10.5 %all_to_all.76 = bf16[16,16,512]{2,1,0:T(8,128)(2,1)S(1)} all-to-all(bf16[16,16,512]{2,1,0:T(8,128)(2,1)S(1)} %broadcast_in_dim.26), channel_id=1, replica_groups=mesh['neuron'=16,'trial'=8] {'neuron'}, dimensions={0} | all-to-all | bytes 524288 | tf_op jit(solution)/shard_map/all_to_all | solution.py:17
  43.7 7.5 %convert_dynamic-update-slice_fusion.5 = (bf16[128,8192]{1,0:T(8,128)(2,1)}, f32[16,8192]{1,0:T(8,128)}, f32[16,8192]{1,0:T(8,128)S(1)}, f32[16,8192]{1,0:T(8,12...) fusion(bf16[128,8192]{1,0:T(8,128)(2,1)} %get-tuple-element.46, f32[16,8192]{1,0:T(8,128)} %copy-done.10, ...), kind=kOutput, calls=%fused_computation.158 | convolution fusion | flops 138936320 | bytes 14303232 | tf_op jit(solution)/shard_map/dot_general | solution.py:60
  56.0 10.5 %all_to_all.77 = bf16[16,16,512]{2,1,0:T(8,128)(2,1)S(1)} all-to-all(bf16[16,16,512]{2,1,0:T(8,128)(2,1)S(1)} %broadcast_in_dim.27), channel_id=1, replica_groups=mesh['neuron'=16,'trial'=8] {'neuron'}, dimensions={0} | all-to-all | bytes 524288 | tf_op jit(solution)/shard_map/all_to_all | solution.py:17
  78.1 10.2 %all_to_all.78 = bf16[16,16,512]{2,1,0:T(8,128)(2,1)S(1)} all-to-all(bf16[16,16,512]{2,1,0:T(8,128)(2,1)S(1)} %broadcast_in_dim.28), channel_id=1, replica_groups=mesh['neuron'=16,'trial'=8] {'neuron'}, dimensions={0} | all-to-all | bytes 524288 | tf_op jit(solution)/shard_map/all_to_all | solution.py:17
  88.3 7.5 %convert_dynamic-update-slice_fusion.3 = (bf16[128,8192]{1,0:T(8,128)(2,1)}, f32[16,8192]{1,0:T(8,128)}, f32[16,8192]{1,0:T(8,128)S(1)}, f32[16,8192]{1,0:T(8,12...) fusion(bf16[128,8192]{1,0:T(8,128)(2,1)} %get-tuple-element.40, f32[16,8192]{1,0:T(8,128)S(1)} %get-tuple-element.41, ...), kind=kOutput, calls=%fused_computation.156 | convolution fusion | flops 138018816 | bytes 14303232 | tf_op jit(solution)/shard_map/dot_general | solution.py:60
  100.4 10.4 %all_to_all.79 = bf16[16,16,512]{2,1,0:T(8,128)(2,1)S(1)} all-to-all(bf16[16,16,512]{2,1,0:T(8,128)(2,1)S(1)} %broadcast_in_dim.29), channel_id=1, replica_groups=mesh['neuron'=16,'trial'=8] {'neuron'}, dimensions={0} | all-to-all | bytes 524288 | tf_op jit(solution)/shard_map/all_to_all | solution.py:17
  134.5 7.5 %convert_dynamic-update-slice_fusion.1 = (bf16[128,8192]{1,0:T(8,128)(2,1)}, f32[16,8192]{1,0:T(8,128)}, f32[16,8192]{1,0:T(8,128)S(1)}, f32[16,8192]{1,0:T(8,12...) fusion(bf16[128,8192]{1,0:T(8,128)(2,1)} %get-tuple-element.34, f32[16,8192]{1,0:T(8,128)} %copy-done.3, ...), kind=kOutput, calls=%fused_computation.154 | convolution fusion | flops 138018816 | bytes 14303232 | tf_op jit(solution)/shard_map/dot_general | solution.py:60
  170.3 10.2 %all_to_all.80 = bf16[16,16,512]{2,1,0:T(8,128)(2,1)S(1)} all-to-all(bf16[16,16,512]{2,1,0:T(8,128)(2,1)S(1)} %broadcast_in_dim.32), channel_id=1, replica_groups=mesh['neuron'=16,'trial'=8] {'neuron'}, dimensions={0} | all-to-all | bytes 524288 | tf_op jit(solution)/shard_map/all_to_all | solution.py:17
  196.1 10.8 %all_to_all.81 = bf16[16,16,512]{2,1,0:T(8,128)(2,1)S(1)} all-to-all(bf16[16,16,512]{2,1,0:T(8,128)(2,1)S(1)} %bitcast.157), channel_id=1, replica_groups=mesh['neuron'=16,'trial'=8] {'neuron'}, dimensions={0} | all-to-all | bytes 524288 | tf_op jit(solution)/shard_map/all_to_all | solution.py:17
  219.8 44.2 %all_to_all.82 = bf16[8,128,1024]{1,2,0:T(8,128)(2,1)} all-to-all(bf16[8,128,1024]{1,2,0:T(8,128)(2,1)} %bitcast.155), channel_id=1, replica_groups=mesh['neuron'=16,'trial'=8] {'trial'}, dimensions={0} | all-to-all | bytes 4194304 | tf_op jit(solution)/shard_map/all_to_all | solution.py:17
  270.8 26.5 %all-to-all-done.11 = bf16[8,256,512]{2,1,0:T(8,128)(2,1)} async-done(((bf16[8,256,512]{2,1,0:T(8,128)(2,1)}), bf16[8,256,512]{2,1,0:T(8,128)(2,1)}, u32[]{:S(2)}, u32[]{:S(2)}) %all-to-all-start.11) | async-done | bytes 2097184 | tf_op jit(solution)/shard_map/all_to_all | solution.py:17
  313.0 16.3 %all-to-all-done.13 = f32[128,4,512]{2,1,0:T(4,128)S(1)} async-done(((f32[128,4,512]{2,1,0:T(4,128)}), f32[128,4,512]{2,1,0:T(4,128)S(1)}, u32[]{:S(2)}, u32[]{:S(2)}) %all-to-all-start.13) | async-done | bytes 1048608 | tf_op jit(solution)/shard_map/all_to_all | solution.py:17
  334.6 26.2 %all-to-all-done.8 = bf16[8,128,1024]{2,1,0:T(8,128)(2,1)} async-done(((bf16[8,128,1024]{2,1,0:T(8,128)(2,1)}), bf16[8,128,1024]{2,1,0:T(8,128)(2,1)}, u32[]{:S(2)}, u32[]{:S(2)}) %all-to-all-start.8) | async-done | bytes 2097184 | tf_op jit(solution)/shard_map/all_to_all | solution.py:17
  371.9 14.4 %all-to-all-done.14 = f32[128,4,512]{2,1,0:T(4,128)} async-done(((f32[128,4,512]{2,1,0:T(4,128)}), f32[128,4,512]{2,1,0:T(4,128)}, u32[]{:S(2)}, u32[]{:S(2)}) %all-to-all-start.14) | async-done | bytes 1048608 | tf_op jit(solution)/shard_map/all_to_all | solution.py:17
  391.7 11.7 %cholesky.104 = f32[128,128]{1,0:T(8,128)S(1)} custom-call(f32[128,128]{1,0:T(8,128)S(1)} %cholesky.266), custom_call_target="Cholesky" | custom-call | tf_op jit(solution)/shard_map/jit(cholesky)/cholesky | solution.py:112
  403.6 9.8 %custom-call.30 = f32[1,128,128]{1,2,0:T(8,128)S(1)} custom-call(f32[1,128,128]{2,1,0:T(8,128)S(1)} %get-tuple-element.65), custom_call_target="InvertDiagBlocksLowerTriangular" | custom-call | tf_op jit(solution)/shard_map/jit(cholesky)/cholesky | solution.py:112
  415.9 11.9 %cholesky.217 = f32[128,128]{1,0:T(8,128)S(1)} custom-call(f32[128,128]{1,0:T(8,128)S(1)} %cholesky.270), custom_call_target="Cholesky" | custom-call | tf_op jit(solution)/shard_map/jit(cholesky)/cholesky | solution.py:112
  427.9 9.8 %custom-call.31 = f32[1,128,128]{1,2,0:T(8,128)S(1)} custom-call(f32[1,128,128]{2,1,0:T(8,128)S(1)} %get-tuple-element.62), custom_call_target="InvertDiagBlocksLowerTriangular" | custom-call | tf_op jit(solution)/shard_map/jit(cholesky)/cholesky | solution.py:112
  439.3 11.7 %cholesky.238 = f32[128,128]{1,0:T(8,128)S(1)} custom-call(f32[128,128]{1,0:T(8,128)S(1)} %cholesky.275), custom_call_target="Cholesky" | custom-call | tf_op jit(solution)/shard_map/jit(cholesky)/cholesky | solution.py:112
  451.7 9.8 %custom-call.32 = f32[1,128,128]{1,2,0:T(8,128)S(1)} custom-call(f32[1,128,128]{2,1,0:T(8,128)S(1)} %get-tuple-element.59), custom_call_target="InvertDiagBlocksLowerTriangular" | custom-call | tf_op jit(solution)/shard_map/jit(cholesky)/cholesky | solution.py:112
  462.9 12.1 %cholesky.255 = f32[128,128]{1,0:T(8,128)S(1)} custom-call(f32[128,128]{1,0:T(8,128)S(1)} %convolution_subtract_fusion.4), custom_call_target="Cholesky" | custom-call | tf_op jit(solution)/shard_map/jit(cholesky)/cholesky | solution.py:112
  480.0 13.8 %while.1 = (s32[]{:T(128)}, f32[512,512]{1,0:T(8,128)}, s32[4,2]{0,1:T(2,128)S(1)}, f32[4,128,128]{2,1,0:T(8,128)}, s32[]{:T(128)}) while((s32[]{:T(128)}, f32[512,512]{1,0:T(8,128)}, s32[4,2]{0,1:T(2,128)S(1)}, f32[4,128,128]{2,1,0:T(8,128)}, s32[]{:T(128)}) %tuple.62), condition=%wide.while_cond, body=%wide.while_body.sunk | while | flops 2 | bytes 132705 | solution.py:113
  493.8 40.1 %custom-call.33 = f32[4,128,128]{1,2,0:T(8,128)S(1)} custom-call(f32[4,128,128]{2,1,0:T(8,128)} %get-tuple-element.9), custom_call_target="InvertDiagBlocksLowerTriangular" | custom-call | tf_op jit(solution)/shard_map/triangular_solve | solution.py:113
  (141 shorter events, 203.6 us)
Async XLA Ops:
  0.6 21.1 %copy-start.7 = (f32[16,8192]{1,0:T(8,128)S(1)}, f32[16,8192]{1,0:T(8,128)}, u32[]{:S(2)}) copy-start(f32[16,8192]{1,0:T(8,128)} %param.13) | copy-start | bytes 1572868
  0.6 21.1 %copy-start.6 = (f32[16,8192]{1,0:T(8,128)S(1)}, f32[16,8192]{1,0:T(8,128)}, u32[]{:S(2)}) copy-start(f32[16,8192]{1,0:T(8,128)} %param.14) | copy-start | bytes 1572868
  0.7 21.1 %copy-start.12 = (f32[8192]{0:T(1024)S(1)}, f32[8192]{0:T(1024)}, u32[]{:S(2)}) copy-start(f32[8192]{0:T(1024)} %param.18) | copy-start | bytes 98308
  0.7 21.1 %copy-start.13 = (f32[8192]{0:T(1024)S(1)}, f32[8192]{0:T(1024)}, u32[]{:S(2)}) copy-start(f32[8192]{0:T(1024)} %param.19) | copy-start | bytes 98308
  0.7 21.1 %copy-start.16 = (f32[16,8192]{1,0:T(8,128)S(1)}, f32[16,8192]{1,0:T(8,128)}, u32[]{:S(2)}) copy-start(f32[16,8192]{1,0:T(8,128)} %param.15) | copy-start | bytes 1572868
  0.7 21.1 %copy-start.14 = (f32[8192]{0:T(1024)S(1)}, f32[8192]{0:T(1024)}, u32[]{:S(2)}) copy-start(f32[8192]{0:T(1024)} %param.16) | copy-start | bytes 98308
  0.7 21.1 %copy-start.15 = (f32[8192]{0:T(1024)S(1)}, f32[8192]{0:T(1024)}, u32[]{:S(2)}) copy-start(f32[8192]{0:T(1024)} %param.17) | copy-start | bytes 98308
  28.4 4.8 copy-start.10
  51.2 15.3 %copy-start.5 = (f32[16,8192]{1,0:T(8,128)}, f32[16,8192]{1,0:T(8,128)S(1)}, u32[]{:S(2)}) copy-start(f32[16,8192]{1,0:T(8,128)S(1)} %get-tuple-element.44) | copy-start | bytes 1572868
  123.4 11.0 %all-to-all-start.5 = ((bf16[16,16,512]{2,1,0:T(8,128)(2,1)}), bf16[16,16,512]{2,1,0:T(8,128)(2,1)S(1)}, u32[]{:S(2)}, u32[]{:S(2)}) async-start(bf16[16,16,512]{2,1,0:T(8,128)(2,1)} %broadcast_in_dim.30), calls=%async_computation.5 | async-start | bytes 524288 | tf_op jit(solution)/shard_map/all_to_all | solution.py:17
  142.0 8.9 %copy-start.4 = (f32[16,8192]{1,0:T(8,128)S(1)}, f32[16,8192]{1,0:T(8,128)}, u32[]{:S(2)}) copy-start(f32[16,8192]{1,0:T(8,128)} %copy-done.3) | copy-start | bytes 1572868
  147.3 11.0 %all-to-all-start.6 = ((bf16[16,16,512]{2,1,0:T(8,128)(2,1)}), bf16[16,16,512]{2,1,0:T(8,128)(2,1)S(1)}, u32[]{:S(2)}, u32[]{:S(2)}) async-start(bf16[16,16,512]{2,1,0:T(8,128)(2,1)} %broadcast_in_dim.31), calls=%async_computation.6 | async-start | bytes 524288 | tf_op jit(solution)/shard_map/all_to_all | solution.py:17
  165.5 4.8 copy-start.9
  165.5 15.0 %copy-start.8 = (f32[16,8192]{1,0:T(8,128)S(1)}, f32[16,8192]{1,0:T(8,128)}, u32[]{:S(2)}) copy-start(f32[16,8192]{1,0:T(8,128)} %get-tuple-element.31) | copy-start | bytes 1572868
  180.6 13.6 %slice-start = ((s8[8388608]{0:T(1024)(128)(4,1)}), s8[4194304]{0:T(1024)(128)(4,1)S(1)}, s32[]{:S(2)}) async-start(s8[8388608]{0:T(1024)(128)(4,1)} %bitcast.151), calls=%async_computation.15 | async-start | bytes 8388608
  188.7 5.5 copy-start
  188.7 5.5 slice-start.1
  188.7 6.0 %copy-start.1 = (bf16[128,8192]{1,0:T(8,128)(2,1)S(1)}, bf16[128,8192]{1,0:T(8,128)(2,1)}, u32[]{:S(2)}) copy-start(bf16[128,8192]{1,0:T(8,128)(2,1)} %get-tuple-element.50) | copy-start | bytes 6291460
  196.1 15.2 %copy-start.2 = (bf16[128,8192]{1,0:T(8,128)(2,1)S(1)}, bf16[128,8192]{1,0:T(8,128)(2,1)}, u32[]{:S(2)}) copy-start(bf16[128,8192]{1,0:T(8,128)(2,1)} %get-tuple-element.50) | copy-start | bytes 6291460
  207.7 12.1 %all-to-all-start.10 = ((bf16[16,16,512]{2,1,0:T(8,128)(2,1)}), bf16[16,16,512]{2,1,0:T(8,128)(2,1)S(1)}, u32[]{:S(2)}, u32[]{:S(2)}) async-start(bf16[16,16,512]{2,1,0:T(8,128)(2,1)} %broadcast_in_dim.33), calls=%async_computation.10 | async-start | bytes 524288 | tf_op jit(solution)/shard_map/all_to_all | solution.py:17
  265.5 31.7 %all-to-all-start.11 = ((bf16[8,256,512]{2,1,0:T(8,128)(2,1)}), bf16[8,256,512]{2,1,0:T(8,128)(2,1)}, u32[]{:S(2)}, u32[]{:S(2)}) async-start(bf16[8,256,512]{2,1,0:T(8,128)(2,1)} %broadcast_in_dim.35), calls=%async_computation.11 | async-start | bytes 4194304 | tf_op jit(solution)/shard_map/all_to_all | solution.py:17
  305.5 23.8 %all-to-all-start.13 = ((f32[128,4,512]{2,1,0:T(4,128)}), f32[128,4,512]{2,1,0:T(4,128)S(1)}, u32[]{:S(2)}, u32[]{:S(2)}) async-start(f32[128,4,512]{2,1,0:T(4,128)} %reshape.107), calls=%async_computation.13 | async-start | bytes 2097152 | tf_op jit(solution)/shard_map/all_to_all | solution.py:17
  329.3 31.5 %all-to-all-start.8 = ((bf16[8,128,1024]{2,1,0:T(8,128)(2,1)}), bf16[8,128,1024]{2,1,0:T(8,128)(2,1)}, u32[]{:S(2)}, u32[]{:S(2)}) async-start(bf16[8,128,1024]{2,1,0:T(8,128)(2,1)} %bitcast.154), calls=%async_computation.8 | async-start | bytes 4194304 | tf_op jit(solution)/shard_map/all_to_all | solution.py:17
  361.9 24.5 %all-to-all-start.14 = ((f32[128,4,512]{2,1,0:T(4,128)}), f32[128,4,512]{2,1,0:T(4,128)}, u32[]{:S(2)}, u32[]{:S(2)}) async-start(f32[128,4,512]{2,1,0:T(4,128)} %broadcast_in_dim.36), calls=%async_computation.14 | async-start | bytes 2097152 | tf_op jit(solution)/shard_map/all_to_all | solution.py:17
  (2 other events, 5.7 us)
